TPU v7x, 128 devices: a whole 4x4x4 slice. The times are simulated.
128 devices in a mesh: heads: 8 (over z, core), width: 4 (over y), sae: 4 (over x).
Axes of the slice: x: 4, y: 4, z: 4, core: 2. Of those that a mesh axis runs over, the one named last changes fastest.
Arguments:
- x_in: bfloat16 [512, 4608], P(None, 'width'), may hold values from -64 to 64
- doc_lengths: int32 [4], replicated, may hold values from 1 to 256, 512 in all
- attn_gain: float32 [4608], P('width'), may hold values from 0.25 to 1.75
- w_query: bfloat16 [4608, 4096], P('width', 'heads'), may hold values from -0.09375 to 0.09375
- w_key: bfloat16 [4608, 2048], P('width', 'heads'), may hold values from -0.09375 to 0.09375
- w_value: bfloat16 [4608, 2048], P('width', 'heads'), may hold values from -0.09375 to 0.09375
- w_out: bfloat16 [4096, 4608], P('heads', 'width'), may hold values from -0.09375 to 0.09375
- post_gain: float32 [4608], replicated, may hold values from 0.25 to 1.75
- enc_weight: bfloat16 [4608, 65536], P(None, ('heads', 'width', 'sae')), may hold values from -0.09375 to 0.09375
- enc_bias: float32 [65536], P(('heads', 'width', 'sae')), may hold values from -1.5 to 0.5
- dec_weight: bfloat16 [65536, 4608], P(('heads', 'width', 'sae')), may hold values from -1 to 1
- dec_bias: float32 [4608], replicated, may hold values from -5 to 5
Outputs:
- grad_enc: bfloat16 [4608, 65536], P(None, ('heads', 'width', 'sae'))
- grad_dec: bfloat16 [65536, 4608], P(('heads', 'width', 'sae'))
- total_loss: float32 [], replicated
Inputs may be any that keep to these rules, and one draw needn't show every extreme that they name: `doc_lengths`: lengths of the 4 documents packed in order; they sum to 512.
All inputs are finite; a program needn't handle non-finite values.
Results may differ from a plain program's by a relative error of at most 0.02.
Values may be sent and summed in bfloat16 or wider, within the bound.
A program may use at most 128 MiB of HBM per device.

v0:
```python
import jax
import jax.numpy as jnp
from jax import lax
from jax.sharding import PartitionSpec as P

D = 4608
HEADS = 32
HEAD_DIM = 128
norm_eps = 1e-06
soft_cap = 50.0
rope_base = 10000.0
l1_weight = 3.0


def rotary(values, position):
    half_dim = values.shape[-1] // 2
    frequency = rope_base ** (-2.0 * jnp.arange(half_dim, dtype=jnp.float32) / values.shape[-1])
    angles = position.astype(jnp.float32)[:, None] * frequency[None, :]
    cosine_table = jnp.cos(angles)[:, None, :]
    sine_table = jnp.sin(angles)[:, None, :]
    first_half = values[..., :half_dim]
    second_half = values[..., half_dim:]
    return jnp.concatenate(
        [
            first_half * cosine_table - second_half * sine_table,
            second_half * cosine_table + first_half * sine_table,
        ],
        axis=-1,
    )


def attend_rows(query_rows, key_rows, value_rows, allowed_rows, scale):
    scores = (
        jnp.einsum("tkgd,skd->kgts", query_rows, key_rows, preferred_element_type=jnp.float32)
        * scale
    )
    capped = soft_cap * jnp.tanh(scores / soft_cap)
    weights = jnp.where(allowed_rows[None, None], jnp.exp(capped), 0.0)
    totals = jnp.sum(weights, axis=-1, keepdims=True)
    probs_bf = (weights / totals).astype(jnp.bfloat16)
    return jnp.einsum(
        "kgts,skd->tkgd", probs_bf, value_rows, preferred_element_type=jnp.float32
    ).astype(jnp.bfloat16)


def per_device(
    x_in,
    doc_lengths,
    attn_gain,
    w_query,
    w_key,
    w_value,
    w_out,
    post_gain,
    enc_weight,
    enc_bias,
    dec_weight,
    dec_bias,
):
    tokens = x_in.shape[0]
    query_heads = w_query.shape[1] // HEAD_DIM
    value_heads = w_key.shape[1] // HEAD_DIM
    boundary = jnp.cumsum(doc_lengths)
    position = jnp.arange(tokens, dtype=jnp.int32)
    segment = jnp.sum((boundary[None, :] <= position[:, None]).astype(jnp.int32), axis=1)
    allowed = (segment[:, None] == segment[None, :]) & (position[None, :] <= position[:, None])
    x_float = x_in.astype(jnp.float32)
    scaled = (x_float * attn_gain).astype(jnp.bfloat16)
    query_part = jnp.dot(scaled, w_query, preferred_element_type=jnp.float32)
    key_part = jnp.dot(scaled, w_key, preferred_element_type=jnp.float32)
    value_part = jnp.dot(scaled, w_value, preferred_element_type=jnp.float32)
    square_part = jnp.sum(x_float * x_float, axis=1)
    query_raw, key_raw, value_raw, square_sums = lax.psum(
        (query_part, key_part, value_part, square_part), "width"
    )
    inverse_rms = lax.rsqrt(square_sums / D + norm_eps)
    query = rotary(
        (query_raw * inverse_rms[:, None]).reshape(tokens, query_heads, HEAD_DIM), position
    ).astype(jnp.bfloat16)
    key_rows = rotary(
        (key_raw * inverse_rms[:, None]).reshape(tokens, value_heads, HEAD_DIM), position
    ).astype(jnp.bfloat16)
    value_rows = (
        (value_raw * inverse_rms[:, None])
        .reshape(tokens, value_heads, HEAD_DIM)
        .astype(jnp.bfloat16)
    )
    query4 = query.reshape(tokens, value_heads, query_heads // value_heads, HEAD_DIM)
    pieces_out = attend_rows(query4, key_rows, value_rows, allowed, (D // HEADS) ** (-0.5))
    mixed = pieces_out.reshape(tokens, query_heads * HEAD_DIM)
    proj_part = jnp.dot(mixed, w_out, preferred_element_type=jnp.float32)
    attn_sum = lax.psum(proj_part, "heads")
    attn_local = attn_sum.astype(jnp.bfloat16)
    attn_proj, x_full = (
        lax.all_gather(attn_local, "width", axis=1, tiled=True),
        lax.all_gather(x_in, "width", axis=1, tiled=True),
    )
    proj_float = attn_proj.astype(jnp.float32)
    inverse_post = lax.rsqrt(jnp.sum(proj_float * proj_float, axis=1) / D + norm_eps)
    resid = (x_full.astype(jnp.float32) + proj_float * inverse_post[:, None] * post_gain).astype(
        jnp.bfloat16
    )
    centered = (resid.astype(jnp.float32) - dec_bias).astype(jnp.bfloat16)
    pre_acts = jnp.dot(centered, enc_weight, preferred_element_type=jnp.float32) + enc_bias
    latent_acts = jnp.maximum(pre_acts, 0.0).astype(jnp.bfloat16)
    row_norms = jnp.sqrt(jnp.sum(jnp.square(dec_weight.astype(jnp.float32)), axis=1) + norm_eps)
    act_sums = jnp.sum(latent_acts.astype(jnp.float32), axis=0)
    penalty_part = jnp.sum(act_sums * row_norms)
    recon_part = jnp.dot(latent_acts, dec_weight, preferred_element_type=jnp.float32)
    recon = lax.psum(recon_part, ("heads", "width", "sae")) + dec_bias
    error = recon - resid.astype(jnp.float32)
    squares_total = jnp.sum(error * error)
    penalty_total = lax.psum(penalty_part, ("heads", "width", "sae"))
    grad_recon = (2.0 / tokens * error).astype(jnp.bfloat16)
    total_loss = (squares_total + l1_weight * penalty_total) / (tokens * D)
    upstream = lax.dot_general(
        grad_recon, dec_weight, (((1,), (1,)), ((), ())), preferred_element_type=jnp.float32
    )
    grad_pre = jnp.where(pre_acts > 0, upstream + l1_weight * row_norms / tokens, 0.0).astype(
        jnp.bfloat16
    )
    grad_enc = lax.dot_general(
        centered, grad_pre, (((0,), (0,)), ((), ())), preferred_element_type=jnp.float32
    ).astype(jnp.bfloat16)
    decoder_term = lax.dot_general(
        latent_acts, grad_recon, (((0,), (0,)), ((), ())), preferred_element_type=jnp.float32
    )
    grad_dec = (
        decoder_term
        + l1_weight
        / tokens
        * act_sums[:, None]
        * dec_weight.astype(jnp.float32)
        / row_norms[:, None]
    ).astype(jnp.bfloat16)
    return (grad_enc, grad_dec, total_loss)


def solution(mesh):
    placed = (
        P(None, "width"),
        P(),
        P("width"),
        P("width", "heads"),
        P("width", "heads"),
        P("width", "heads"),
        P("heads", "width"),
        P(),
        P(None, ("heads", "width", "sae")),
        P(("heads", "width", "sae")),
        P(("heads", "width", "sae"), None),
        P(),
    )
    return jax.shard_map(
        per_device,
        mesh=mesh,
        in_specs=placed,
        out_specs=(P(None, ("heads", "width", "sae")), P(("heads", "width", "sae"), None), P()),
        check_vma=False,
    )
```

profile of v0, /device:TPU:1, one launch (start us, length us, event | category | flops | bytes accessed | tf_op | source)
XLA Modules:
  0.0 471.6 jit_solution(9375944868353371698)
XLA Ops:
  7.2 0.0 copy-start
  7.2 0.0 all-reduce.7.cloned.1.call-start
  7.3 3.6 fusion.23
  10.9 2.7 fusion.25
  13.6 1.3 fusion.27
  14.9 0.0 all-reduce.7.cloned.1.call-update
  15.0 0.0 all-gather.5.cloned.1.call-start
  15.0 0.2 reduce-window.8
  15.2 0.3 fusion.14
  15.5 9.5 %psum.50 = f32[512]{0:T(512)S(1)} all-reduce(f32[512]{0:T(512)S(1)} %fusion.14), channel_id=1, replica_groups=mesh['heads'=8,'width'=4,'sae'=4] {'width'}, use_global_device_ids=true, to_apply=%region_2.3 | all-reduce | flops 512 | bytes 4096 | tf_op jit(solution)/shard_map/psum | solution.py:73
  25.1 0.1 convert_reduce_fusion.1
  25.2 0.9 fusion.22
  26.1 1.7 multiply_cosine_fusion
  27.8 49.0 %all-reduce.7.cloned.1.call-done = (f32[512,256]{1,0:T(8,128)}, f32[512,512]{1,0:T(8,128)}, f32[512,256]{1,0:T(8,128)}) async-done(((f32[512,256]{1,0:T(8,128)}, f32[512,512]{1,0:T(8,128)}, f32[512,256]{1,0:T(8,128)}), (f32[512,256]{1,0:T(8,128)}, f32[512,512]{1,0:T(8,128)}, f32[512,256]{1,0:T(8,128)})) %all-reduce.7.cloned.1.call-update) | async-done | bytes 2097168 | tf_op jit(solution)/shard_map/psum | solution.py:73
  76.9 2.1 broadcast_multiply_fusion.1
  78.9 0.3 reshape.168
  79.2 1.5 fusion.40
  80.7 1.4 broadcast_multiply_fusion
  82.1 0.4 reshape.169
  82.5 1.8 subtract_convert_fusion
  84.3 0.1 copy.23
  84.3 0.1 copy.24
  84.4 0.1 copy.30
  84.6 1.3 subtract_convert_fusion.1
  85.9 2.9 fusion.12
  88.8 1.6 fusion.21
  90.4 0.9 fusion.41
  91.3 52.5 %all-reduce.8 = bf16[512,1152]{1,0:T(8,128)(2,1)} all-reduce(f32[512,1152]{1,0:T(8,128)S(1)} %fusion.41), channel_id=1, replica_groups=mesh['heads'=8,'width'=4,'sae'=4] {'heads'}, use_global_device_ids=true, to_apply=%region_8.9 | all-reduce | flops 589824 | bytes 3538944 | tf_op jit(solution)/shard_map/psum | solution.py:92
  143.8 0.0 all-gather.5.cloned.1.call-update
  143.8 0.0 all-gather.3.cloned.1.call-start
  143.8 0.7 all-gather.3.cloned.1.call-update
  144.5 0.2 all-reduce.5.cloned.1.call-start
  144.8 51.8 %all-gather.5.cloned.1.call-done = bf16[512,4608]{1,0:T(8,128)(2,1)} async-done(((bf16[512,1152]{1,0:T(8,128)(2,1)}), bf16[512,4608]{1,0:T(8,128)(2,1)}) %all-gather.5.cloned.1.call-update) | async-done | bytes 4718608 | tf_op jit(solution)/shard_map/all_gather | solution.py:95
  196.6 3.3 fusion
  200.0 51.3 %all-gather.3.cloned.1.call-done = bf16[512,4608]{1,0:T(8,128)(2,1)} async-done(((bf16[512,1152]{1,0:T(8,128)(2,1)}), bf16[512,4608]{1,0:T(8,128)(2,1)}) %all-gather.3.cloned.1.call-update) | async-done | bytes 4718608 | tf_op jit(solution)/shard_map/all_gather | solution.py:96
  251.3 5.9 %fusion.3 = bf16[512,4608]{1,0:T(8,128)(2,1)S(1)} fusion(bf16[512,4608]{1,0:T(8,128)(2,1)} %all-gather.5.cloned.1.call-done, bf16[512,4608]{1,0:T(8,128)(2,1)} %all-gather.3.cloned.1.call-done, f32[4608]{0:T(1024)S(1)} %copy-done.8, f32[512]{0:T(512)S(1)} %add_rsqrt_fusion), kind=kLoop, calls=%fused_computation.9 | loop fusion | flops 14155776 | bytes 14176256 | tf_op jit(solution)/shard_map/convert_element_type | solution.py:100
  257.2 0.0 slice-start.1
  257.3 6.4 %convert_reduce_fusion = (f32[512]{0:T(512)S(1)}, f32[512,512]{1,0:T(8,128)S(1)}) fusion(f32[512]{0:T(512)S(1)} %copy-done.12, bf16[4608,512]{1,0:T(8,128)(2,1)} %param.20, bf16[512,4608]{1,0:T(8,128)(2,1)S(1)} %fusion.3, f32[4608]{0:T(1024)S(1)} %copy-done.9), kind=kOutput, calls=%fused_computation.32 | convolution fusion | flops 2424045056 | bytes 10508288 | tf_op jit(solution)/shard_map/dot_general | solution.py:104
  263.7 5.1 %fusion.39 = f32[512,4608]{1,0:T(8,128)} fusion(bf16[512,4608]{1,0:T(8,128)(2,1)S(1)} %bitcast.41, f32[512,512]{1,0:T(8,128)S(1)} %get-tuple-element.25), kind=kOutput, calls=%fused_computation.69 | convolution fusion | flops 2416443392 | bytes 15204352 | tf_op jit(solution)/shard_map/dot_general | solution.py:109
  268.8 0.0 all-reduce.5.cloned.1.call-update
  268.8 3.3 fusion.5
  272.2 0.6 multiply_reduce_fusion.1
  272.8 65.8 %psum.55 = f32[]{:T(128)} all-reduce(f32[]{:T(128)} %get-tuple-element.16), channel_id=1, replica_groups=mesh['heads'=8,'width'=4,'sae'=4] {'heads','width','sae'}, use_global_device_ids=true, to_apply=%region_15.16 | all-reduce | flops 1 | bytes 8 | tf_op jit(solution)/shard_map/psum | solution.py:113
  339.2 94.4 %all-reduce.5.cloned.1.call-done = f32[512,4608]{1,0:T(8,128)} async-done(((f32[512,4608]{1,0:T(8,128)}), f32[512,4608]{1,0:T(8,128)}) %all-reduce.5.cloned.1.call-update) | async-done | bytes 9437200 | tf_op jit(solution)/shard_map/psum | solution.py:110
  433.6 8.4 %multiply_reduce_fusion = (f32[]{:T(128)}, bf16[512,4608]{1,0:T(8,128)(2,1)S(1)}) fusion(bf16[512,4608]{1,0:T(8,128)(2,1)} %copy-done.2, f32[512,4608]{1,0:T(8,128)} %all-reduce.5.cloned.1.call-done, f32[4608]{0:T(1024)S(1)} %copy-done.9), kind=kLoop, calls=%fused_computation.15 | loop fusion | flops 16515071 | bytes 18892804 | tf_op jit(solution)/shard_map/reduce_sum | solution.py:112
  442.0 6.7 %fusion.20 = bf16[512,512]{1,0:T(8,128)(2,1)S(1)} fusion(bf16[512,4608]{1,0:T(8,128)(2,1)S(1)} %get-tuple-element.7, bf16[512,4608]{1,0:T(8,128)(2,1)} %param.22, f32[512,512]{1,0:T(8,128)S(1)} %get-tuple-element.25, f32[512]{0:T(512)S(1)} %get-tuple-element.17), kind=kOutput, calls=%fused_computation.30 | convolution fusion | flops 2416967680 | bytes 11012096 | tf_op jit(solution)/shard_map/dot_general | solution.py:116
  448.7 6.8 %convolution_convert_fusion = bf16[4608,512]{1,0:T(8,128)(2,1)} fusion(bf16[512,512]{1,0:T(8,128)(2,1)S(1)} %fusion.20, bf16[512,4608]{1,0:T(8,128)(2,1)} %copy-done.2, f32[4608]{0:T(1024)S(1)} %copy-done.9), kind=kOutput, calls=%fused_computation.17 | convolution fusion | flops 2425356288 | bytes 9979904 | tf_op jit(solution)/shard_map/dot_general | solution.py:122
  456.1 7.8 %fusion.8 = bf16[512,4608]{1,0:T(8,128)(2,1)} fusion(bf16[512,4608]{1,0:T(8,128)(2,1)} %param.22, bf16[512,4608]{1,0:T(8,128)(2,1)} %copy-done.4, f32[512]{0:T(512)S(1)} %get-tuple-element.18, f32[512]{0:T(512)S(1)} %get-tuple-element.19, f32[512,512]{1,0:T(8,128)S(1)} %get-tuple-element.25), kind=kOutput, calls=%fused_computation.14 | convolution fusion | flops 2428239872 | bytes 15208448 | tf_op jit(solution)/shard_map/dot_general | solution.py:125
  (35 shorter events, 0.1 us)
Async XLA Ops:
  7.2 83.3 %copy-start = (bf16[512,1152]{1,0:T(8,128)(2,1)S(1)}, bf16[512,1152]{1,0:T(8,128)(2,1)}, u32[]{:S(2)}) copy-start(bf16[512,1152]{1,0:T(8,128)(2,1)} %param.18) | copy-start | bytes 3538948
  7.2 6.5 %copy-start.3 = (bf16[512,1152]{1,0:T(8,128)(2,1)S(1)}, bf16[512,1152]{1,0:T(8,128)(2,1)}, u32[]{:S(2)}) copy-start(bf16[512,1152]{1,0:T(8,128)(2,1)} %param.12) | copy-start | bytes 3538948
  7.2 6.4 %copy-start.11 = (f32[1152]{0:T(1024)S(1)}, f32[1152]{0:T(1024)}, u32[]{:S(2)}) copy-start(f32[1152]{0:T(1024)} %param.14) | copy-start | bytes 13828
  7.2 6.4 %copy-start.10 = (bf16[1152,256]{1,0:T(8,128)(2,1)S(1)}, bf16[1152,256]{1,0:T(8,128)(2,1)}, u32[]{:S(2)}) copy-start(bf16[1152,256]{1,0:T(8,128)(2,1)} %param.17) | copy-start | bytes 1769476
  7.2 7.8 %copy-start.13 = (s32[4]{0:T(128)S(1)}, s32[4]{0:T(128)}, u32[]{:S(2)}) copy-start(s32[4]{0:T(128)} %param.13) | copy-start | bytes 52
  7.2 69.6 %all-reduce.7.cloned.1.call-start = ((), (), s32[]{:S(2)}) async-start(), calls=%async_computation.3 | async-start | bytes 4194304 | tf_op jit(solution)/shard_map/psum | solution.py:73
  15.0 181.6 %all-gather.5.cloned.1.call-start = ((), (), s32[]{:S(2)}) async-start(), calls=%async_computation.1 | async-start | bytes 5898240 | tf_op jit(solution)/shard_map/all_gather | solution.py:95
  82.4 2.0 copy-start.6
  82.4 2.1 copy-start.5
  85.9 2.9 copy-start.7
  91.3 160.0 %copy-start.8 = (f32[4608]{0:T(1024)S(1)}, f32[4608]{0:T(1024)}, u32[]{:S(2)}) copy-start(f32[4608]{0:T(1024)} %param.19) | copy-start | bytes 55300
  143.8 107.5 %all-gather.3.cloned.1.call-start = ((), (), s32[]{:S(2)}) async-start(), calls=%async_computation | async-start | bytes 5898240 | tf_op jit(solution)/shard_map/all_gather | solution.py:96
  144.5 289.1 %all-reduce.5.cloned.1.call-start = ((), (), s32[]{:S(2)}) async-start(), calls=%async_computation.2 | async-start | bytes 18874368 | tf_op jit(solution)/shard_map/psum | solution.py:110
  199.9 57.3 %copy-start.9 = (f32[4608]{0:T(1024)S(1)}, f32[4608]{0:T(1024)}, u32[]{:S(2)}) copy-start(f32[4608]{0:T(1024)} %param.23) | copy-start | bytes 55300
  199.9 57.3 %copy-start.12 = (f32[512]{0:T(512)S(1)}, f32[512]{0:T(512)}, u32[]{:S(2)}) copy-start(f32[512]{0:T(512)} %param.21) | copy-start | bytes 6148
  251.3 12.4 %slice-start = ((s8[4718592]{0:T(1024)(128)(4,1)}), s8[4194304]{0:T(1024)(128)(4,1)S(1)}, s32[]{:S(2)}) async-start(s8[4718592]{0:T(1024)(128)(4,1)} %bitcast.40), calls=%async_computation.4 | async-start | bytes 8388608
  257.2 6.4 %copy-start.2 = (bf16[512,4608]{1,0:T(8,128)(2,1)}, bf16[512,4608]{1,0:T(8,128)(2,1)S(1)}, u32[]{:S(2)}) copy-start(bf16[512,4608]{1,0:T(8,128)(2,1)S(1)} %fusion.3) | copy-start | bytes 14155780
  257.2 6.5 %slice-start.1 = ((s8[4718592]{0:T(1024)(128)(4,1)}), s8[524288]{0:T(1024)(128)(4,1)S(1)}, s32[]{:S(2)}) async-start(s8[4718592]{0:T(1024)(128)(4,1)} %bitcast.40), calls=%async_computation.5 | async-start | bytes 1048576
  442.0 6.7 %copy-start.4 = (bf16[512,4608]{1,0:T(8,128)(2,1)}, bf16[512,4608]{1,0:T(8,128)(2,1)S(1)}, u32[]{:S(2)}) copy-start(bf16[512,4608]{1,0:T(8,128)(2,1)S(1)} %get-tuple-element.7) | copy-start | bytes 14155780
  456.1 7.9 %copy-start.1 = (bf16[512,1152]{1,0:T(8,128)(2,1)S(1)}, bf16[512,1152]{1,0:T(8,128)(2,1)}, u32[]{:S(2)}) copy-start(bf16[512,1152]{1,0:T(8,128)(2,1)} %param.18) | copy-start | bytes 3538948
Sparse Core Ops, SparseCore 0:
  15.1 61.7 all-reduce.6
  143.9 52.6 all-gather.4
  198.3 52.9 all-gather.2
  268.9 164.6 all-reduce.4
where the time goes:
time: 472 us
  waiting for transfers between devices  247 us (52%)
  blocking collectives  128 us (27%)
  matrix products  45.7 us (10%)
  other arithmetic  31.4 us (7%)
  between operations  16.5 us (3%)
    psum x1, waiting for transfers between devices, per_device(): recon = lax.psum(recon_part, ('heads', 'width', 'sae')) + dec_bias  94.4 us
    psum x1, blocking collectives, per_device(): penalty_total = lax.psum(penalty_part, ('heads', 'width', 'sae'))  65.8 us
    psum x1, blocking collectives, per_device(): attn_sum = lax.psum(proj_part, 'heads')  52.5 us
    all_gather x1, waiting for transfers between devices, per_device(): lax.all_gather(attn_local, 'width', axis=1, tiled=True)  51.8 us
    all_gather x1, waiting for transfers between devices, per_device(): lax.all_gather(x_in, 'width', axis=1, tiled=True)  51.3 us
    psum x1, waiting for transfers between devices, per_device(): lax.psum((query_part, key_part, value_part, square_part), 'width')  49 us
    psum x1, blocking collectives, per_device(): lax.psum((query_part, key_part, value_part, square_part), 'width')  9.54 us
  transfers between devices with their start and end apart: 4, of which 4 were waited for; matrix products, arithmetic and copies ran while one was open for 2% of the time, Pallas kernels for 0%

commit v1 on v0

--- a/solution.py
+++ b/solution.py
@@ -89,7 +89,11 @@
     pieces_out = attend_rows(query4, key_rows, value_rows, allowed, (D // HEADS) ** (-0.5))
     mixed = pieces_out.reshape(tokens, query_heads * HEAD_DIM)
     proj_part = jnp.dot(mixed, w_out, preferred_element_type=jnp.float32)
-    attn_sum = lax.psum(proj_part, "heads")
+    n_dev = lax.axis_size("heads")
+    attn_sum, far = (proj_part, 1)
+    while far < n_dev:
+        attn_sum = attn_sum + lax.ppermute(attn_sum, "heads", [(i, i ^ far) for i in range(n_dev)])
+        far = 2 * far
     attn_local = attn_sum.astype(jnp.bfloat16)
     attn_proj, x_full = (
         lax.all_gather(attn_local, "width", axis=1, tiled=True),

time: 472 us -> 533 us (1.13)
  waiting for transfers between devices: 247 us -> 354 us
  blocking collectives: 128 us -> 75.4 us
    ppermute x0 -> x3, waiting for transfers between devices: none -> 106 us  [per_device(): lax.ppermute(attn_sum, 'heads', [(i, i ^ far) for i in range(n_dev)])]
    psum x1 -> x0, blocking collectives: 52.5 us -> none  [per_device(): attn_sum = lax.psum(proj_part, 'heads')]
  transfers between devices with their start and end apart: 4 -> 7, of which waited for: 4 -> 7; matrix products, arithmetic and copies ran while one was open for 2% -> 2% of each run, Pallas kernels for 0% -> 0%
where the time goes in v1:
time: 533 us
  waiting for transfers between devices  354 us (66%)
  blocking collectives  75.4 us (14%)
  matrix products  45.7 us (9%)
  other arithmetic  33 us (6%)
  between operations  16.5 us (3%)
  starting transfers between devices  5.56 us (1%)
    ppermute x3, waiting for transfers between devices, per_device(): lax.ppermute(attn_sum, 'heads', [(i, i ^ far) for i in range(n_dev)])  106 us
    psum x1, waiting for transfers between devices, per_device(): recon = lax.psum(recon_part, ('heads', 'width', 'sae')) + dec_bias  94.4 us
    psum x1, blocking collectives, per_device(): penalty_total = lax.psum(penalty_part, ('heads', 'width', 'sae'))  65.8 us
    all_gather x1, waiting for transfers between devices, per_device(): lax.all_gather(attn_local, 'width', axis=1, tiled=True)  52.8 us
    all_gather x1, waiting for transfers between devices, per_device(): lax.all_gather(x_in, 'width', axis=1, tiled=True)  51.3 us
    psum x1, waiting for transfers between devices, per_device(): lax.psum((query_part, key_part, value_part, square_part), 'width')  49 us
  transfers between devices with their start and end apart: 7, of which 7 were waited for; matrix products, arithmetic and copies ran while one was open for 2% of the time, Pallas kernels for 0%

profile of v1, /device:TPU:1, one launch (start us, length us, event | category | flops | bytes accessed | tf_op | source)
XLA Modules:
  0.0 532.5 jit_solution(4236732112478832288)
XLA Ops:
  7.3 3.6 fusion.21
  10.9 2.7 fusion.23
  13.6 1.3 fusion.25
  15.0 0.2 reduce-window.8
  15.2 0.3 fusion.14
  15.5 9.5 %psum.43 = f32[512]{0:T(512)S(1)} all-reduce(f32[512]{0:T(512)S(1)} %fusion.14), channel_id=1, replica_groups=mesh['heads'=8,'width'=4,'sae'=4] {'width'}, use_global_device_ids=true, to_apply=%region_2.3 | all-reduce | flops 512 | bytes 4096 | tf_op jit(solution)/shard_map/psum | solution.py:73
  25.1 0.1 convert_reduce_fusion.1
  25.2 0.9 fusion.20
  26.1 1.7 multiply_cosine_fusion
  27.8 49.0 %all-reduce.6.cloned.1.call-done = (f32[512,256]{1,0:T(8,128)}, f32[512,512]{1,0:T(8,128)}, f32[512,256]{1,0:T(8,128)}) async-done(((f32[512,256]{1,0:T(8,128)}, f32[512,512]{1,0:T(8,128)}, f32[512,256]{1,0:T(8,128)}), (f32[512,256]{1,0:T(8,128)}, f32[512,512]{1,0:T(8,128)}, f32[512,256]{1,0:T(8,128)})) %all-reduce.6.cloned.1.call-update) | async-done | bytes 2097168 | tf_op jit(solution)/shard_map/psum | solution.py:73
  76.8 2.0 broadcast_multiply_fusion.1
  78.9 0.3 reshape.168
  79.2 1.5 fusion.40
  80.7 1.4 broadcast_multiply_fusion
  82.0 0.4 reshape.169
  82.4 1.8 subtract_convert_fusion
  84.2 0.1 copy.23
  84.3 0.1 copy.24
  84.4 0.1 copy.30
  84.6 1.3 subtract_convert_fusion.1
  85.9 2.9 fusion.12
  88.8 1.6 fusion.19
  90.4 0.9 fusion.41
  91.3 0.9 collective-permute-start
  92.2 4.2 collective-permute-done
  96.4 0.2 add.82
  96.6 1.4 collective-permute-start.1
  98.0 51.2 %collective-permute-done.1 = f32[512,1152]{1,0:T(8,128)S(1)} collective-permute-done((f32[512,1152]{1,0:T(8,128)S(1)}, f32[512,1152]{1,0:T(8,128)S(1)}, u32[]{:S(2)}, u32[]{:S(2)}) %collective-permute-start.1) | collective-permute-done | bytes 2359328 | tf_op jit(solution)/shard_map/ppermute | solution.py:95
  149.1 0.2 add.83
  149.4 2.9 collective-permute-start.2
  152.3 50.2 %collective-permute-done.2 = f32[512,1152]{1,0:T(8,128)S(1)} collective-permute-done((f32[512,1152]{1,0:T(8,128)S(1)}, f32[512,1152]{1,0:T(8,128)S(1)}, u32[]{:S(2)}, u32[]{:S(2)}) %collective-permute-start.2) | collective-permute-done | bytes 2359328 | tf_op jit(solution)/shard_map/ppermute | solution.py:95
  202.5 1.2 add_convert_fusion
  203.8 0.7 all-gather.3.cloned.1.call-update
  204.5 0.2 all-reduce.4.cloned.1.call-start
  204.7 52.8 %all-gather.5.cloned.1.call-done = bf16[512,4608]{1,0:T(8,128)(2,1)} async-done(((bf16[512,1152]{1,0:T(8,128)(2,1)}), bf16[512,4608]{1,0:T(8,128)(2,1)}) %all-gather.5.cloned.1.call-update) | async-done | bytes 4718608 | tf_op jit(solution)/shard_map/all_gather | solution.py:99
  257.5 3.3 fusion
  260.9 51.3 %all-gather.3.cloned.1.call-done = bf16[512,4608]{1,0:T(8,128)(2,1)} async-done(((bf16[512,1152]{1,0:T(8,128)(2,1)}), bf16[512,4608]{1,0:T(8,128)(2,1)}) %all-gather.3.cloned.1.call-update) | async-done | bytes 4718608 | tf_op jit(solution)/shard_map/all_gather | solution.py:100
  312.2 5.9 %fusion.3 = bf16[512,4608]{1,0:T(8,128)(2,1)S(1)} fusion(bf16[512,4608]{1,0:T(8,128)(2,1)} %all-gather.5.cloned.1.call-done, bf16[512,4608]{1,0:T(8,128)(2,1)} %all-gather.3.cloned.1.call-done, f32[4608]{0:T(1024)S(1)} %copy-done.8, f32[512]{0:T(512)S(1)} %add_rsqrt_fusion), kind=kLoop, calls=%fused_computation.9 | loop fusion | flops 14155776 | bytes 14176256 | tf_op jit(solution)/shard_map/convert_element_type | solution.py:104
  318.2 6.4 %convert_reduce_fusion = (f32[512]{0:T(512)S(1)}, f32[512,512]{1,0:T(8,128)S(1)}) fusion(f32[512]{0:T(512)S(1)} %copy-done.12, bf16[4608,512]{1,0:T(8,128)(2,1)} %param.20, bf16[512,4608]{1,0:T(8,128)(2,1)S(1)} %fusion.3, f32[4608]{0:T(1024)S(1)} %copy-done.9), kind=kOutput, calls=%fused_computation.31 | convolution fusion | flops 2424045056 | bytes 10508288 | tf_op jit(solution)/shard_map/dot_general | solution.py:108
  324.6 5.1 fusion.39
  329.7 3.3 fusion.5
  333.1 0.6 multiply_reduce_fusion.1
  333.7 65.8 %psum.47 = f32[]{:T(128)} all-reduce(f32[]{:T(128)} %get-tuple-element.16), channel_id=1, replica_groups=mesh['heads'=8,'width'=4,'sae'=4] {'heads','width','sae'}, use_global_device_ids=true, to_apply=%region_14.15 | all-reduce | flops 1 | bytes 8 | tf_op jit(solution)/shard_map/psum | solution.py:117
  400.2 94.4 %all-reduce.4.cloned.1.call-done = f32[512,4608]{1,0:T(8,128)} async-done(((f32[512,4608]{1,0:T(8,128)}), f32[512,4608]{1,0:T(8,128)}) %all-reduce.4.cloned.1.call-update) | async-done | bytes 9437200 | tf_op jit(solution)/shard_map/psum | solution.py:114
  494.6 8.4 %multiply_reduce_fusion = (f32[]{:T(128)}, bf16[512,4608]{1,0:T(8,128)(2,1)S(1)}) fusion(bf16[512,4608]{1,0:T(8,128)(2,1)} %copy-done.2, f32[512,4608]{1,0:T(8,128)} %all-reduce.4.cloned.1.call-done, f32[4608]{0:T(1024)S(1)} %copy-done.9), kind=kLoop, calls=%fused_computation.15 | loop fusion | flops 16515071 | bytes 18892804 | tf_op jit(solution)/shard_map/reduce_sum | solution.py:116
  502.9 6.7 %convolution_add_fusion = bf16[512,512]{1,0:T(8,128)(2,1)S(1)} fusion(bf16[512,4608]{1,0:T(8,128)(2,1)S(1)} %get-tuple-element.7, bf16[512,4608]{1,0:T(8,128)(2,1)} %param.22, f32[512]{0:T(512)S(1)} %get-tuple-element.17), kind=kOutput, calls=%fused_computation.29 | convolution fusion | flops 2416443392 | bytes 9963520 | tf_op jit(solution)/shard_map/dot_general | solution.py:120
  509.6 6.8 %convolution_convert_fusion = bf16[4608,512]{1,0:T(8,128)(2,1)} fusion(bf16[512,4608]{1,0:T(8,128)(2,1)} %copy-done.2, f32[4608]{0:T(1024)S(1)} %copy-done.9, bf16[512,512]{1,0:T(8,128)(2,1)S(1)} %convolution_add_fusion, f32[512,512]{1,0:T(8,128)S(1)} %get-tuple-element.25), kind=kOutput, calls=%fused_computation.17 | convolution fusion | flops 2425880576 | bytes 11028480 | tf_op jit(solution)/shard_map/dot_general | solution.py:126
  517.0 7.8 %fusion.8 = bf16[512,4608]{1,0:T(8,128)(2,1)} fusion(bf16[512,4608]{1,0:T(8,128)(2,1)} %param.22, bf16[512,4608]{1,0:T(8,128)(2,1)} %copy-done.4, f32[512]{0:T(512)S(1)} %get-tuple-element.18, f32[512]{0:T(512)S(1)} %get-tuple-element.19, f32[512,512]{1,0:T(8,128)S(1)} %get-tuple-element.25), kind=kOutput, calls=%fused_computation.14 | convolution fusion | flops 2428239872 | bytes 15208448 | tf_op jit(solution)/shard_map/dot_general | solution.py:129
  (43 shorter events, 0.3 us)
Async XLA Ops:
  7.2 83.2 %copy-start = (bf16[512,1152]{1,0:T(8,128)(2,1)S(1)}, bf16[512,1152]{1,0:T(8,128)(2,1)}, u32[]{:S(2)}) copy-start(bf16[512,1152]{1,0:T(8,128)(2,1)} %param.18) | copy-start | bytes 3538948
  7.2 6.4 %copy-start.3 = (bf16[512,1152]{1,0:T(8,128)(2,1)S(1)}, bf16[512,1152]{1,0:T(8,128)(2,1)}, u32[]{:S(2)}) copy-start(bf16[512,1152]{1,0:T(8,128)(2,1)} %param.12) | copy-start | bytes 3538948
  7.2 6.4 %copy-start.11 = (f32[1152]{0:T(1024)S(1)}, f32[1152]{0:T(1024)}, u32[]{:S(2)}) copy-start(f32[1152]{0:T(1024)} %param.14) | copy-start | bytes 13828
  7.2 6.4 %copy-start.10 = (bf16[1152,256]{1,0:T(8,128)(2,1)S(1)}, bf16[1152,256]{1,0:T(8,128)(2,1)}, u32[]{:S(2)}) copy-start(bf16[1152,256]{1,0:T(8,128)(2,1)} %param.17) | copy-start | bytes 1769476
  7.2 7.8 %copy-start.13 = (s32[4]{0:T(128)S(1)}, s32[4]{0:T(128)}, u32[]{:S(2)}) copy-start(s32[4]{0:T(128)} %param.13) | copy-start | bytes 52
  7.2 69.6 %all-reduce.6.cloned.1.call-start = ((), (), s32[]{:S(2)}) async-start(), calls=%async_computation.3 | async-start | bytes 4194304 | tf_op jit(solution)/shard_map/psum | solution.py:73
  15.0 242.6 %all-gather.5.cloned.1.call-start = ((), (), s32[]{:S(2)}) async-start(), calls=%async_computation.1 | async-start | bytes 5898240 | tf_op jit(solution)/shard_map/all_gather | solution.py:99
  82.4 2.0 copy-start.6
  82.4 2.1 copy-start.5
  85.9 2.9 copy-start.7
  91.3 5.1 collective-permute-start
  96.6 52.5 %collective-permute-start.1 = (f32[512,1152]{1,0:T(8,128)S(1)}, f32[512,1152]{1,0:T(8,128)S(1)}, u32[]{:S(2)}, u32[]{:S(2)}) collective-permute-start(f32[512,1152]{1,0:T(8,128)S(1)} %add.82), channel_id=1, source_target_pairs={{0,32},{16,48},{32,0},{48,16},{64,96},{80,112},{96,64},{112,80},{1... | collective-permute-start | bytes 7077896 | tf_op jit(solution)/shard_map/ppermute | solution.py:95
  149.4 53.2 %collective-permute-start.2 = (f32[512,1152]{1,0:T(8,128)S(1)}, f32[512,1152]{1,0:T(8,128)S(1)}, u32[]{:S(2)}, u32[]{:S(2)}) collective-permute-start(f32[512,1152]{1,0:T(8,128)S(1)} %add.83), channel_id=1, source_target_pairs={{0,64},{16,80},{32,96},{48,112},{64,0},{80,16},{96,32},{112,48},{1... | collective-permute-start | bytes 7077896 | tf_op jit(solution)/shard_map/ppermute | solution.py:95
  203.8 108.5 %copy-start.8 = (f32[4608]{0:T(1024)S(1)}, f32[4608]{0:T(1024)}, u32[]{:S(2)}) copy-start(f32[4608]{0:T(1024)} %param.19) | copy-start | bytes 55300
  203.8 108.5 %all-gather.3.cloned.1.call-start = ((), (), s32[]{:S(2)}) async-start(), calls=%async_computation | async-start | bytes 5898240 | tf_op jit(solution)/shard_map/all_gather | solution.py:100
  204.5 290.0 %all-reduce.4.cloned.1.call-start = ((), (), s32[]{:S(2)}) async-start(), calls=%async_computation.2 | async-start | bytes 18874368 | tf_op jit(solution)/shard_map/psum | solution.py:114
  260.9 57.3 %copy-start.9 = (f32[4608]{0:T(1024)S(1)}, f32[4608]{0:T(1024)}, u32[]{:S(2)}) copy-start(f32[4608]{0:T(1024)} %param.23) | copy-start | bytes 55300
  260.9 57.3 %copy-start.12 = (f32[512]{0:T(512)S(1)}, f32[512]{0:T(512)}, u32[]{:S(2)}) copy-start(f32[512]{0:T(512)} %param.21) | copy-start | bytes 6148
  312.2 12.4 %slice-start = ((s8[4718592]{0:T(1024)(128)(4,1)}), s8[4194304]{0:T(1024)(128)(4,1)S(1)}, s32[]{:S(2)}) async-start(s8[4718592]{0:T(1024)(128)(4,1)} %bitcast.39), calls=%async_computation.4 | async-start | bytes 8388608
  318.2 6.4 %copy-start.2 = (bf16[512,4608]{1,0:T(8,128)(2,1)}, bf16[512,4608]{1,0:T(8,128)(2,1)S(1)}, u32[]{:S(2)}) copy-start(bf16[512,4608]{1,0:T(8,128)(2,1)S(1)} %fusion.3) | copy-start | bytes 14155780
  318.2 6.4 %slice-start.1 = ((s8[4718592]{0:T(1024)(128)(4,1)}), s8[524288]{0:T(1024)(128)(4,1)S(1)}, s32[]{:S(2)}) async-start(s8[4718592]{0:T(1024)(128)(4,1)} %bitcast.39), calls=%async_computation.5 | async-start | bytes 1048576
  502.9 6.7 %copy-start.4 = (bf16[512,4608]{1,0:T(8,128)(2,1)}, bf16[512,4608]{1,0:T(8,128)(2,1)S(1)}, u32[]{:S(2)}) copy-start(bf16[512,4608]{1,0:T(8,128)(2,1)S(1)} %get-tuple-element.7) | copy-start | bytes 14155780
  517.0 7.9 %copy-start.1 = (bf16[512,1152]{1,0:T(8,128)(2,1)S(1)}, bf16[512,1152]{1,0:T(8,128)(2,1)}, u32[]{:S(2)}) copy-start(bf16[512,1152]{1,0:T(8,128)(2,1)} %param.18) | copy-start | bytes 3538948
Sparse Core Ops, SparseCore 0:
  15.1 61.7 all-reduce.5
  203.9 53.5 all-gather.4
  259.2 52.9 all-gather.2
  329.9 164.6 all-reduce.3
